TPU v7x, 32 devices: a whole 2x2x4 slice. The times are simulated.
32 devices in a mesh: dp: 2 (over y), ctx: 4 (over z), exp: 4 (over x, core).
Axes of the slice: x: 2, y: 2, z: 4, core: 2. Of those that a mesh axis runs over, the one named last changes fastest.
Arguments:
- queries: bfloat16 [8, 512, 2048], P(('dp', 'exp'), 'ctx'), may hold values from -24 to 24
- keys: bfloat16 [8, 512, 2048], P(('dp', 'exp'), 'ctx'), may hold values from -20 to 20
- values: bfloat16 [8, 512, 2048], P(('dp', 'exp'), 'ctx'), may hold values from -6 to 6
- resid: bfloat16 [8, 512, 2048], P(('dp', 'exp'), 'ctx'), may hold values from -3 to 3
- norm_gain: float32 [2048], replicated, may hold values from 0.5 to 1.5
- expert_ids: int32 [8, 512, 8], P(('dp', 'exp'), 'ctx'), may hold values from 0 to 15, all different within a row; in each aligned block of 128 rows (0 to 127, 128 to 255, ..., all dimensions but the last counted through in order) at most 68 rows name the same one
- gate_weights: float32 [8, 512, 8], P(('dp', 'exp'), 'ctx'), may hold values from 0.05 to 0.5
- mask_flags: int32 [8, 512], P(('dp', 'exp'), 'ctx'), may hold values 0 or 1
- cotangent: bfloat16 [8, 512, 2048], P(('dp', 'exp'), 'ctx'), may hold values from -0.59765625 to 0.59765625
- w_gate_up: bfloat16 [16, 2048, 1024], P(('ctx', 'exp')), may hold values from -0.125 to 0.125
- w_down: bfloat16 [16, 2048, 512], P(('ctx', 'exp')), may hold values from -0.25 to 0.25
Outputs:
- stream: bfloat16 [8, 512, 2048], P(('dp', 'exp'), 'ctx')
- grad_gate_up: float32 [16, 2048, 1024], P(('ctx', 'exp'), 'dp')
- grad_down: float32 [16, 2048, 512], P(('ctx', 'exp'), 'dp')
Inputs may be any that keep to these rules, and one draw needn't show every extreme that they name: `expert_ids`: in the rows of one device no expert is named more than 68 times, and some device names some expert exactly 68 times.
All inputs are finite; a program needn't handle non-finite values. No bound on the sum of `mask_flags` on one device may be relied on, other than what follows from the above.
Results may differ from a plain program's by a relative error of at most 0.0088.
Values may be sent and summed in bfloat16 or wider, within the bound.
No kernel may reach another device: no remote copies, remote signals or barrier semaphores. Data moves between devices by JAX's collectives and lax.ppermute only.
A program may use at most 128 MiB of HBM per device.

v0:
```python
import math
import jax
import jax.numpy as jnp
from jax import lax
from jax.sharding import PartitionSpec as P

HEADS = 16
HEAD_DIM = 128


def attend(query_rows, keys_all, values_all):
    tokens = query_rows.shape[0]
    length = keys_all.shape[0]
    query_heads = query_rows.reshape(tokens, HEADS, HEAD_DIM)
    key_heads = keys_all.reshape(length, HEADS, HEAD_DIM)
    value_heads = values_all.reshape(length, HEADS, HEAD_DIM)
    scale_factor = 1.0 / math.sqrt(HEAD_DIM)
    scores = (
        jnp.einsum("qhd,khd->hqk", query_heads, key_heads, preferred_element_type=jnp.float32)
        * scale_factor
    )
    largest = jnp.max(scores, axis=2, keepdims=True)
    powers = jnp.exp(scores - largest)
    probs = (powers / jnp.sum(powers, axis=2, keepdims=True)).astype(jnp.bfloat16)
    attended = jnp.einsum("hqk,khd->qhd", probs, value_heads, preferred_element_type=jnp.float32)
    return attended.reshape(tokens, HEADS * HEAD_DIM)


def rms_normed(stream, norm_gain):
    widened = lax.optimization_barrier(stream).astype(jnp.float32)
    factor = lax.rsqrt(jnp.mean(widened * widened, axis=-1, keepdims=True) + 1e-05)
    return (widened * factor * norm_gain).astype(jnp.bfloat16)


def slot_targets(routes, experts, capacity):
    flat_ids = routes.reshape(-1)
    onehot = (flat_ids[:, None] == jnp.arange(experts, dtype=jnp.int32)[None, :]).astype(jnp.int32)
    ranks = jnp.cumsum(onehot, axis=0) - 1
    within = jnp.sum(ranks * onehot, axis=1)
    return flat_ids * capacity + within


def pack_rows(normed, cot_rows, routes, gates, flags, experts, capacity):
    tokens = normed.shape[0]
    model_width = normed.shape[1]
    top_count = routes.shape[1]
    targets = slot_targets(routes, experts, capacity)
    scaled = (
        cot_rows.astype(jnp.float32)[:, None, :]
        * gates[:, :, None]
        * flags.astype(jnp.float32)[:, None, None]
    )
    grad_rows = scaled.astype(jnp.bfloat16).reshape(tokens * top_count, model_width)
    input_rows = jnp.repeat(normed, top_count, axis=0)
    empty = jnp.zeros((experts * capacity, model_width), jnp.bfloat16)
    return (empty.at[targets].set(input_rows), empty.at[targets].set(grad_rows))


def expert_term(input_rows, grad_rows, gate_up, down_map):
    hidden_width = down_map.shape[1]
    projected = jnp.dot(input_rows, gate_up, preferred_element_type=jnp.float32)
    gate_part = projected[:, :hidden_width]
    up_part = projected[:, hidden_width:]
    sigma = jax.nn.sigmoid(gate_part)
    activated = gate_part * sigma
    hidden = (activated * up_part).astype(jnp.bfloat16)
    back_hidden = jnp.dot(grad_rows, down_map, preferred_element_type=jnp.float32)
    slope = sigma * (1.0 + gate_part * (1.0 - sigma))
    back_both = jnp.concatenate(
        [back_hidden * up_part * slope, back_hidden * activated], axis=1
    ).astype(jnp.bfloat16)
    return (hidden, back_both)


def term_rows(input_rows, grad_rows, hidden, back_both):
    contract = (((0,), (0,)), ((), ()))
    left_part = lax.dot_general(input_rows, back_both, contract, preferred_element_type=jnp.float32)
    right_part = lax.dot_general(grad_rows, hidden, contract, preferred_element_type=jnp.float32)
    return jnp.concatenate([left_part, right_part], axis=1)


def per_device(
    queries,
    keys,
    values,
    resid,
    norm_gain,
    expert_ids,
    gate_weights,
    mask_flags,
    cotangent,
    w_gate_up,
    w_down,
):
    keys_all, values_all = (
        lax.all_gather(keys, "ctx", axis=1, tiled=True),
        lax.all_gather(values, "ctx", axis=1, tiled=True),
    )
    attended = attend(queries[0], keys_all[0], values_all[0])
    stream = (resid[0].astype(jnp.float32) + attended).astype(jnp.bfloat16)
    normed = rms_normed(stream, norm_gain)
    ctx_count = lax.axis_size("ctx")
    exp_count = lax.axis_size("exp")
    experts = ctx_count * exp_count
    tokens = queries.shape[1]
    capacity = min(tokens, tokens * expert_ids.shape[2] * 17 // (16 * experts))
    model_width = normed.shape[1]
    input_buf, grad_buf = pack_rows(
        normed, cotangent[0], expert_ids[0], gate_weights[0], mask_flags[0], experts, capacity
    )
    block_shape = (experts, capacity, model_width)
    arrived = (
        lax.all_to_all(
            input_buf.reshape(block_shape), ("ctx", "exp"), split_axis=0, concat_axis=0, tiled=True
        ),
        lax.all_to_all(
            grad_buf.reshape(block_shape), ("ctx", "exp"), split_axis=0, concat_axis=0, tiled=True
        ),
    )
    input_rows = arrived[0].reshape(-1, model_width)
    grad_rows = arrived[1].reshape(-1, model_width)
    hidden, back_both = expert_term(input_rows, grad_rows, w_gate_up[0], w_down[0])
    summed = lax.psum_scatter(
        term_rows(input_rows, grad_rows, hidden, back_both).astype(jnp.bfloat16),
        "dp",
        scatter_dimension=0,
        tiled=True,
    ).astype(jnp.float32)
    hidden_width = w_down.shape[2]
    return (stream[None], summed[:, : 2 * hidden_width][None], summed[:, 2 * hidden_width :][None])


def solution(mesh):
    placed = (
        P(("dp", "exp"), "ctx", None),
        P(("dp", "exp"), "ctx", None),
        P(("dp", "exp"), "ctx", None),
        P(("dp", "exp"), "ctx", None),
        P(),
        P(("dp", "exp"), "ctx", None),
        P(("dp", "exp"), "ctx", None),
        P(("dp", "exp"), "ctx"),
        P(("dp", "exp"), "ctx", None),
        P(("ctx", "exp"), None, None),
        P(("ctx", "exp"), None, None),
    )
    return jax.shard_map(
        per_device,
        mesh=mesh,
        in_specs=placed,
        out_specs=(
            P(("dp", "exp"), "ctx", None),
            P(("ctx", "exp"), "dp", None),
            P(("ctx", "exp"), "dp", None),
        ),
        check_vma=False,
    )
```

profile of v0, /device:TPU:0, one launch (start us, length us, event | category | flops | bytes accessed | tf_op | source)
XLA Modules:
  0.0 449.8 jit_solution(16724601727391645695)
XLA Ops:
  7.2 0.7 all-gather.5.cloned.1.call-update
  7.9 0.7 broadcast_multiply_fusion
  8.6 0.8 copy.28
  9.6 0.7 convert_bitcast_fusion.1
  10.2 0.1 copy.27
  10.3 0.1 mul.100
  10.6 4.5 %reduce-window.6 = s32[16,8,128]{2,1,0:T(8,128)S(1)} reduce-window(s32[16,8,128]{2,1,0:T(8,128)S(1)} %fusion.37, s32[]{:T(128)} %constant.8.clone.1), window={size=1x1x128 pad=0_0x0_0x127_0}, to_apply=%region_2.0 | reduce-window | flops 2080768 | bytes 131076 | tf_op jit(solution)/shard_map/reduce-window
  15.2 0.1 copy.30
  15.6 0.8 copy.33
  16.4 1.1 bitcast_convert_fusion
  17.6 9.7 %scatter_custom_fusion.1 = bf16[1088,2048]{1,0:T(8,128)(2,1)} fusion(s32[1024]{0:T(1024)S(1)} %bitcast.80, f32[1024]{0:T(1024)S(1)} %mul.113, f32[1024]{0:T(1024)S(1)} %mul.109, f32[128,2048]{1,0:T(8,128)S(1)} %bitcast_convert_fusion, bf16[]{:T(256)} %constant.6.clone.1), kind=kCustom, calls=%fused_computation.7 | custom fusion | flops 6291456 | bytes 5513218 | tf_op jit(solution)/shard_map/scatter | solution.py:56
  27.3 7.1 %reshape.112 = bf16[16,68,2048]{2,1,0:T(8,128)(2,1)} reshape(bf16[1088,2048]{1,0:T(8,128)(2,1)} %scatter_custom_fusion.1) | data formatting | bytes 8912896 | tf_op jit(solution)/shard_map/reshape | solution.py:117
  34.4 7.6 %all-to-all-start.1 = ((bf16[16,68,2048]{2,1,0:T(8,128)(2,1)}), bf16[16,68,2048]{2,1,0:T(8,128)(2,1)}, u32[]{:S(2)}, u32[]{:S(2)}) async-start(bf16[16,68,2048]{2,1,0:T(8,128)(2,1)} %reshape.112), calls=%async_computation.1 | async-start | bytes 9437184 | tf_op jit(solution)/shard_map/all_to_all | solution.py:116
  42.0 0.2 all-gather.3.cloned.1.call-start
  42.2 1.0 copy.22
  43.3 0.1 copy.37
  43.4 46.5 %all-gather.5.cloned.1.call-done = bf16[1,512,2048]{2,1,0:T(8,128)(2,1)} async-done(((bf16[1,128,2048]{2,1,0:T(8,128)(2,1)}), bf16[1,512,2048]{2,1,0:T(8,128)(2,1)}) %all-gather.5.cloned.1.call-update) | async-done | bytes 2097168 | tf_op jit(solution)/shard_map/all_gather | solution.py:97
  89.9 3.9 copy.25
  93.8 78.7 %all-gather.3.cloned.1.call-done = bf16[1,512,2048]{1,2,0:T(8,128)(2,1)} async-done(((bf16[1,128,2048]{1,2,0:T(8,128)(2,1)}), bf16[1,512,2048]{1,2,0:T(8,128)(2,1)}) %all-gather.3.cloned.1.call-update) | async-done | bytes 2097168 | tf_op jit(solution)/shard_map/all_gather | solution.py:96
  172.5 2.3 fusion.32
  174.8 1.4 fusion.48
  176.2 0.6 copy-done.2
  176.8 7.9 %fusion.25 = f32[16,128,128]{1,2,0:T(8,128)S(1)} fusion(bf16[512,16,128]{0,2,1:T(8,128)(2,1)} %bitcast.74, f32[16,128]{1,0:T(8,128)S(1)} %fusion.48, f32[16,128,512]{2,1,0:T(8,128)} %copy-done.2), kind=kOutput, calls=%fused_computation.37 | convolution fusion | flops 273680896 | bytes 7348224 | tf_op jit(solution)/shard_map/hqk,khd->qhd/dot_general | solution.py:25
  184.8 1.3 copy.32
  186.1 1.5 fusion.28
  187.5 0.2 fusion.29
  187.7 1.0 fusion.31
  188.7 9.6 %scatter_custom_fusion = bf16[1088,2048]{1,0:T(8,128)(2,1)} fusion(s32[1024]{0:T(1024)S(1)} %bitcast.81, bf16[]{:T(256)} %constant.6.clone.1, bf16[128,2048]{1,0:T(8,128)(2,1)} %fusion.31), kind=kCustom, calls=%fused_computation.11 | custom fusion | bytes 4980738 | tf_op jit(solution)/shard_map/scatter | solution.py:56
  198.4 7.0 %reshape.110 = bf16[16,68,2048]{2,1,0:T(8,128)(2,1)} reshape(bf16[1088,2048]{1,0:T(8,128)(2,1)} %scatter_custom_fusion) | data formatting | bytes 8912896 | tf_op jit(solution)/shard_map/reshape | solution.py:114
  205.4 9.0 %all-to-all-start = ((bf16[16,68,2048]{2,1,0:T(8,128)(2,1)}), bf16[16,68,2048]{2,1,0:T(8,128)(2,1)}, u32[]{:S(2)}, u32[]{:S(2)}) async-start(bf16[16,68,2048]{2,1,0:T(8,128)(2,1)} %reshape.110), calls=%async_computation | async-start | bytes 9437184 | tf_op jit(solution)/shard_map/all_to_all | solution.py:113
  214.3 0.3 reduce-scatter.2.cloned.1.call-start
  214.6 7.1 %reshape.113 = bf16[1088,2048]{1,0:T(8,128)(2,1)} reshape(bf16[16,68,2048]{2,1,0:T(8,128)(2,1)} %all-to-all-done.1) | data formatting | bytes 8912896 | tf_op jit(solution)/shard_map/reshape | solution.py:121
  221.7 79.4 %all-to-all-done = bf16[16,68,2048]{2,1,0:T(8,128)(2,1)} async-done(((bf16[16,68,2048]{2,1,0:T(8,128)(2,1)}), bf16[16,68,2048]{2,1,0:T(8,128)(2,1)}, u32[]{:S(2)}, u32[]{:S(2)}) %all-to-all-start) | async-done | bytes 4456480 | tf_op jit(solution)/shard_map/all_to_all | solution.py:113
  301.2 7.1 %reshape.111 = bf16[1088,2048]{1,0:T(8,128)(2,1)} reshape(bf16[16,68,2048]{2,1,0:T(8,128)(2,1)} %all-to-all-done) | data formatting | bytes 8912896 | tf_op jit(solution)/shard_map/reshape | solution.py:120
  308.2 8.0 %fusion.5 = f32[1088,1024]{1,0:T(8,128)S(1)} fusion(bf16[1088,2048]{1,0:T(8,128)(2,1)} %reshape.111, bf16[1,2048,1024]{2,1,0:T(8,128)(2,1)} %param.20), kind=kOutput, calls=%fused_computation.9 | convolution fusion | flops 4563402752 | bytes 13107200 | tf_op jit(solution)/shard_map/dot_general | solution.py:61
  316.3 4.3 convolution_convert_fusion.1
  320.6 3.3 multiply_convert_fusion.2
  323.9 6.2 %convolution_convert_fusion = bf16[2048,1024]{0,1:T(8,128)(2,1)S(1)} fusion(bf16[1088,2048]{1,0:T(8,128)(2,1)S(1)} %bitcast.70, bf16[1088,512]{1,0:T(8,128)(2,1)S(1)} %get-tuple-element.10, bf16[1088,512]{1,0:T(8,128)(2,1)S(1)} %get-tuple-element.9), kind=kOutput, calls=%fused_computation.18 | convolution fusion | flops 4569956352 | bytes 10878976 | tf_op jit(solution)/shard_map/dot_general | solution.py:77
  330.2 3.7 pad_maximum_fusion
  333.9 0.3 copy.26
  334.3 0.7 copy-done.4
  334.9 0.9 fusion.26
  335.8 92.3 %reduce-scatter.2.cloned.1.call-done = bf16[1024,1536]{0,1:T(8,128)(2,1)} async-done(((bf16[2048,1536]{0,1:T(8,128)(2,1)}), bf16[1024,1536]{0,1:T(8,128)(2,1)}) %reduce-scatter.2.cloned.1.call-update) | async-done | bytes 3145744 | tf_op jit(solution)/shard_map/reduce_scatter | solution.py:123
  428.1 2.6 convert_element_type.76
  430.8 1.6 slice_bitcast_fusion.1
  432.3 2.5 slice_bitcast_fusion
  434.9 5.5 %copy.34 = f32[1,1024,1024]{2,1,0:T(8,128)} copy(f32[1,1024,1024]{1,2,0:T(8,128)} %slice_bitcast_fusion) | data formatting | bytes 8388608
  440.3 2.9 copy.35
  (42 shorter events, 0.9 us)
Async XLA Ops:
  7.2 313.4 %copy-start = (bf16[1,2048,512]{2,1,0:T(8,128)(2,1)S(1)}, bf16[1,2048,512]{2,1,0:T(8,128)(2,1)}, u32[]{:S(2)}) copy-start(bf16[1,2048,512]{2,1,0:T(8,128)(2,1)} %param.21) | copy-start | bytes 6291460
  7.2 82.7 %all-gather.5.cloned.1.call-start = ((), (), s32[]{:S(2)}) async-start(), calls=%async_computation.4 | async-start | bytes 2621440 | tf_op jit(solution)/shard_map/all_gather | solution.py:97
  34.4 7.8 %copy-start.5 = (bf16[1,128,2048]{2,1,0:T(8,128)(2,1)S(1)}, bf16[1,128,2048]{2,1,0:T(8,128)(2,1)}, u32[]{:S(2)}) copy-start(bf16[1,128,2048]{2,1,0:T(8,128)(2,1)} %param.12) | copy-start | bytes 1572868
  34.4 8.8 %copy-start.6 = (bf16[1,128,2048]{2,1,0:T(8,128)(2,1)S(1)}, bf16[1,128,2048]{2,1,0:T(8,128)(2,1)}, u32[]{:S(2)}) copy-start(bf16[1,128,2048]{2,1,0:T(8,128)(2,1)} %param.11) | copy-start | bytes 1572868
  34.4 170.9 %all-to-all-start.1 = ((bf16[16,68,2048]{2,1,0:T(8,128)(2,1)}), bf16[16,68,2048]{2,1,0:T(8,128)(2,1)}, u32[]{:S(2)}, u32[]{:S(2)}) async-start(bf16[16,68,2048]{2,1,0:T(8,128)(2,1)} %reshape.112), calls=%async_computation.1 | async-start | bytes 9437184 | tf_op jit(solution)/shard_map/all_to_all | solution.py:116
  42.0 130.5 %all-gather.3.cloned.1.call-start = ((), (), s32[]{:S(2)}) async-start(), calls=%async_computation.3 | async-start | bytes 2621440 | tf_op jit(solution)/shard_map/all_gather | solution.py:96
  174.8 2.0 copy-start.2
  184.7 3.0 copy-start.7
  205.4 95.8 %all-to-all-start = ((bf16[16,68,2048]{2,1,0:T(8,128)(2,1)}), bf16[16,68,2048]{2,1,0:T(8,128)(2,1)}, u32[]{:S(2)}, u32[]{:S(2)}) async-start(bf16[16,68,2048]{2,1,0:T(8,128)(2,1)} %reshape.110), calls=%async_computation | async-start | bytes 9437184 | tf_op jit(solution)/shard_map/all_to_all | solution.py:113
  214.3 213.8 %reduce-scatter.2.cloned.1.call-start = ((), (), s32[]{:S(2)}) async-start(), calls=%async_computation.5 | async-start | bytes 9437184 | tf_op jit(solution)/shard_map/reduce_scatter | solution.py:123
  301.1 15.1 %slice-start = ((s8[4456448]{0:T(1024)(128)(4,1)}), s8[262144]{0:T(1024)(128)(4,1)S(1)}, s32[]{:S(2)}) async-start(s8[4456448]{0:T(1024)(128)(4,1)} %bitcast.67), calls=%async_computation.6 | async-start | bytes 524288
  308.2 8.0 %slice-start.1 = ((s8[4456448]{0:T(1024)(128)(4,1)}), s8[4194304]{0:T(1024)(128)(4,1)S(1)}, s32[]{:S(2)}) async-start(s8[4456448]{0:T(1024)(128)(4,1)} %bitcast.67), calls=%async_computation.7 | async-start | bytes 8388608
  316.2 7.6 %slice-start.2 = ((s8[4456448]{0:T(1024)(128)(4,1)}), s8[4194304]{0:T(1024)(128)(4,1)S(1)}, s32[]{:S(2)}) async-start(s8[4456448]{0:T(1024)(128)(4,1)} %bitcast.69), calls=%async_computation.8 | async-start | bytes 8388608
  320.6 3.3 slice-start.3
  323.9 6.3 %copy-start.3 = (bf16[2048,512]{0,1:T(8,128)(2,1)S(1)}, bf16[2048,512]{0,1:T(8,128)(2,1)}, u32[]{:S(2)}) copy-start(bf16[2048,512]{0,1:T(8,128)(2,1)} %convolution_convert_fusion.1) | copy-start | bytes 6291460
  333.9 1.0 copy-start.4
  434.9 8.4 %copy-start.1 = (bf16[1,2048,512]{2,1,0:T(8,128)(2,1)S(1)}, bf16[1,2048,512]{2,1,0:T(8,128)(2,1)}, u32[]{:S(2)}) copy-start(bf16[1,2048,512]{2,1,0:T(8,128)(2,1)} %param.21) | copy-start | bytes 6291460
Sparse Core Ops, SparseCore 0:
  9.6 80.2 all-gather.4
  92.0 80.4 all-gather.2
  334.0 94.0 reduce-scatter.1
where the time goes:
time: 451 us; the launch traced here: 450 us
  waiting for transfers between devices  298 us (66%)
  local copies, waits for them, and re-layouts  61 us (14%)
  matrix products  32 us (7%)
  other arithmetic  28.1 us (6%)
  starting transfers between devices  17 us (4%)
  between operations  14 us (3%)
    reduce_scatter x1, waiting for transfers between devices, per_device(): lax.psum_scatter(term_rows(input_rows, grad_rows, hidden, back_both).asty...  92.3 us
    all_to_all x1, waiting for transfers between devices, per_device(): lax.all_to_all(input_buf.reshape(block_shape), ('ctx', 'exp'), split_axis...  79.4 us
    all_gather x1, waiting for transfers between devices, per_device(): lax.all_gather(keys, 'ctx', axis=1, tiled=True)  78.7 us
    all_gather x1, waiting for transfers between devices, per_device(): lax.all_gather(values, 'ctx', axis=1, tiled=True)  46.5 us
    unnamed x30, local copies, waits for them, and re-layouts  12.4 us
    scatter x1, other arithmetic, pack_rows(): return (empty.at[targets].set(input_rows), empty.at[targets].set(grad_rows))  9.65 us
    scatter x1, local copies, waits for them, and re-layouts, pack_rows(): return (empty.at[targets].set(input_rows), empty.at[targets].set(grad_rows))  9.63 us
  transfers between devices with their start and end apart: 5, of which 4 were waited for; matrix products, arithmetic and copies ran while one was open for 16% of the time, Pallas kernels for 0%

commit v1 on v0

--- a/solution.py
+++ b/solution.py
@@ -1,11 +1,32 @@
+import functools
 import math
 import jax
 import jax.numpy as jnp
 from jax import lax
 from jax.sharding import PartitionSpec as P
+from jax.lax import axis_index, axis_size, ppermute
 
 HEADS = 16
 HEAD_DIM = 128
+
+
+def list_sectors(patch, shard_axis):
+    front, later, all_rows = (axis_size(shard_axis), axis_index(shard_axis), patch.shape[1])
+    series = [tick * front if d == 1 else tick for d, tick in enumerate(patch.shape)]
+    w2 = lax.dynamic_update_slice_in_dim(
+        jnp.zeros(series, patch.dtype), patch, later * all_rows, axis=1
+    )
+    carry = y2 = patch
+    for dev in range(1, front // 2 + 1):
+        carry = ppermute(carry, shard_axis, list(map(lambda d: (d, (d + 1) % front), range(front))))
+        w2 = lax.dynamic_update_slice_in_dim(w2, carry, (later - dev) % front * all_rows, axis=1)
+        if 2 * dev < front:
+            y2 = ppermute(y2, shard_axis, list(map(lambda d: (d, (d - 1) % front), range(front))))
+            w2 = lax.dynamic_update_slice_in_dim(w2, y2, (later + dev) % front * all_rows, axis=1)
+    return w2
+
+
+_change_side = functools.partial(list_sectors, shard_axis="ctx")
 
 
 def attend(query_rows, keys_all, values_all):
@@ -92,10 +113,7 @@
     w_gate_up,
     w_down,
 ):
-    keys_all, values_all = (
-        lax.all_gather(keys, "ctx", axis=1, tiled=True),
-        lax.all_gather(values, "ctx", axis=1, tiled=True),
-    )
+    keys_all, values_all = (_change_side(keys), lax.all_gather(values, "ctx", axis=1, tiled=True))
     attended = attend(queries[0], keys_all[0], values_all[0])
     stream = (resid[0].astype(jnp.float32) + attended).astype(jnp.bfloat16)
     normed = rms_normed(stream, norm_gain)

time: 451 us -> 495 us (1.098)
  starting transfers between devices: 17 us -> 52.1 us
  local copies, waits for them, and re-layouts: 61 us -> 70.5 us
    ppermute x0 -> x3, waiting for transfers between devices: none -> 126 us  [the longest x2 126 us: list_sectors(): ppermute(carry, shard_axis, list(map(lambda d: (d, (d + 1) % front), rang...]
    all_gather x1 -> x0, waiting for transfers between devices: 78.7 us -> none  [per_device(): lax.all_gather(keys, 'ctx', axis=1, tiled=True)]
    all_gather x1, waiting for transfers between devices: 46.5 us -> 0.01 us  [per_device(): lax.all_gather(values, 'ctx', axis=1, tiled=True)]
    ppermute x0 -> x3, starting transfers between devices: none -> 37.4 us  [the longest x2 35.5 us: list_sectors(): ppermute(carry, shard_axis, list(map(lambda d: (d, (d + 1) % front), rang...]
    dynamic_update_slice x0 -> x4, local copies, waits for them, and re-layouts: none -> 6.44 us  [the longest x2 3.74 us: list_sectors(): lax.dynamic_update_slice_in_dim(w2, carry, (later - dev) % front * all_ro...]
    unnamed x30 -> x28, local copies, waits for them, and re-layouts: 12.4 us -> 14.1 us
  transfers between devices with their start and end apart: 5 -> 7, of which waited for: 4 -> 4; matrix products, arithmetic and copies ran while one was open for 16% -> 10% of each run, Pallas kernels for 0% -> 0%
where the time goes in v1:
time: 495 us; the launch traced here: 493 us
  waiting for transfers between devices  298 us (60%)
  local copies, waits for them, and re-layouts  70.5 us (14%)
  starting transfers between devices  52.1 us (11%)
  matrix products  30.1 us (6%)
  other arithmetic  27.9 us (6%)
  between operations  14.3 us (3%)
    ppermute x2, waiting for transfers between devices, list_sectors(): ppermute(carry, shard_axis, list(map(lambda d: (d, (d + 1) % front), rang...  126 us
    reduce_scatter x1, waiting for transfers between devices, per_device(): lax.psum_scatter(term_rows(input_rows, grad_rows, hidden, back_both).asty...  92.4 us
    all_to_all x1, waiting for transfers between devices, per_device(): lax.all_to_all(input_buf.reshape(block_shape), ('ctx', 'exp'), split_axis...  79.5 us
    ppermute x2, starting transfers between devices, list_sectors(): ppermute(carry, shard_axis, list(map(lambda d: (d, (d + 1) % front), rang...  35.5 us
    unnamed x28, local copies, waits for them, and re-layouts  14.1 us
  transfers between devices with their start and end apart: 7, of which 4 were waited for; matrix products, arithmetic and copies ran while one was open for 10% of the time, Pallas kernels for 0%

profile of v1, /device:TPU:0, one launch (start us, length us, event | category | flops | bytes accessed | tf_op | source)
XLA Modules:
  0.0 493.1 jit_solution(18416686503206618369)
XLA Ops:
  7.2 0.8 broadcast_multiply_fusion
  8.0 0.8 copy.32
  9.0 0.7 convert_bitcast_fusion.1
  10.0 4.5 reduce-window.6
  15.0 0.8 copy.37
  15.9 1.1 bitcast_convert_fusion
  17.1 9.7 %scatter_custom_fusion.1 = bf16[1088,2048]{1,0:T(8,128)(2,1)} fusion(s32[1024]{0:T(1024)S(1)} %bitcast.98, f32[1024]{0:T(1024)S(1)} %mul.133, f32[1024]{0:T(1024)S(1)} %mul.129, f32[128,2048]{1,0:T(8,128)S(1)} %bitcast_convert_fusion, bf16[]{:T(256)} %constant.46.clone.1), kind=kCustom, calls=%fused_computation.7 | custom fusion | flops 6291456 | bytes 5513218 | tf_op jit(solution)/shard_map/scatter | solution.py:77
  26.7 7.1 %reshape.112 = bf16[16,68,2048]{2,1,0:T(8,128)(2,1)} reshape(bf16[1088,2048]{1,0:T(8,128)(2,1)} %scatter_custom_fusion.1) | data formatting | bytes 8912896 | tf_op jit(solution)/shard_map/reshape | solution.py:135
  33.8 7.5 %all-to-all-start.1 = ((bf16[16,68,2048]{2,1,0:T(8,128)(2,1)}), bf16[16,68,2048]{2,1,0:T(8,128)(2,1)}, u32[]{:S(2)}, u32[]{:S(2)}) async-start(bf16[16,68,2048]{2,1,0:T(8,128)(2,1)} %reshape.112), calls=%async_computation.1 | async-start | bytes 9437184 | tf_op jit(solution)/shard_map/all_to_all | solution.py:134
  41.4 0.7 all-gather.2.cloned.1.call-update
  42.4 1.9 collective-permute-start
  44.3 2.0 collective-permute-start.1
  46.3 121.5 %collective-permute-done = bf16[1,128,2048]{1,2,0:T(8,128)(2,1)} collective-permute-done((bf16[1,128,2048]{1,2,0:T(8,128)(2,1)S(1)}, bf16[1,128,2048]{1,2,0:T(8,128)(2,1)}, u32[]{:S(2)}, u32[]{:S(2)}) %collective-permute-start) | collective-permute-done | bytes 524320 | tf_op jit(solution)/shard_map/ppermute | solution.py:21
  167.8 33.5 %collective-permute-start.2 = (bf16[1,128,2048]{1,2,0:T(8,128)(2,1)}, bf16[1,128,2048]{1,2,0:T(8,128)(2,1)}, u32[]{:S(2)}, u32[]{:S(2)}) collective-permute-start(bf16[1,128,2048]{1,2,0:T(8,128)(2,1)} %collective-permute-done), channel_id=1, source_target_pairs={{0,4},{4,8},{8,12},{12,0},{1,5},{5,9},{9,13},{13,1},{2,6},{6,10},{... | collective-permute-start | bytes 1572872 | tf_op jit(solution)/shard_map/ppermute | solution.py:21
  201.3 1.5 broadcast_in_dim.10
  202.8 0.8 constant_dynamic-update-slice_fusion.3
  203.6 1.1 copy.42
  204.8 1.9 constant_dynamic-update-slice_fusion.2
  206.6 1.9 constant_dynamic-update-slice_fusion.1
  208.5 4.1 collective-permute-done.2
  212.6 1.9 constant_dynamic-update-slice_fusion
  214.5 2.4 fusion.34
  216.9 2.0 copy-done.2
  218.9 1.1 fusion.50
  220.0 3.9 copy.28
  223.9 5.9 %fusion.27 = f32[16,128,128]{1,2,0:T(8,128)S(1)} fusion(bf16[512,16,128]{0,2,1:T(8,128)(2,1)} %bitcast.92, f32[16,128]{1,0:T(8,128)S(1)} %fusion.50, f32[16,512,128]{2,1,0:T(8,128)} %copy-done.2), kind=kOutput, calls=%fused_computation.39 | convolution fusion | flops 273680896 | bytes 7348224 | tf_op jit(solution)/shard_map/hqk,khd->qhd/dot_general | solution.py:46
  229.8 1.3 copy.36
  231.1 1.5 fusion.30
  232.8 1.0 fusion.33
  233.8 9.6 %scatter_custom_fusion = bf16[1088,2048]{1,0:T(8,128)(2,1)} fusion(s32[1024]{0:T(1024)S(1)} %bitcast.99, bf16[]{:T(256)} %constant.46.clone.1, bf16[128,2048]{1,0:T(8,128)(2,1)} %fusion.33), kind=kCustom, calls=%fused_computation.11 | custom fusion | bytes 4980738 | tf_op jit(solution)/shard_map/scatter | solution.py:77
  243.4 7.0 %reshape.110 = bf16[16,68,2048]{2,1,0:T(8,128)(2,1)} reshape(bf16[1088,2048]{1,0:T(8,128)(2,1)} %scatter_custom_fusion) | data formatting | bytes 8912896 | tf_op jit(solution)/shard_map/reshape | solution.py:132
  250.5 6.8 %all-to-all-start = ((bf16[16,68,2048]{2,1,0:T(8,128)(2,1)}), bf16[16,68,2048]{2,1,0:T(8,128)(2,1)}, u32[]{:S(2)}, u32[]{:S(2)}) async-start(bf16[16,68,2048]{2,1,0:T(8,128)(2,1)} %reshape.110), calls=%async_computation | async-start | bytes 9437184 | tf_op jit(solution)/shard_map/all_to_all | solution.py:131
  257.6 7.1 %reshape.113 = bf16[1088,2048]{1,0:T(8,128)(2,1)} reshape(bf16[16,68,2048]{2,1,0:T(8,128)(2,1)} %all-to-all-done.1) | data formatting | bytes 8912896 | tf_op jit(solution)/shard_map/reshape | solution.py:139
  264.6 79.5 %all-to-all-done = bf16[16,68,2048]{2,1,0:T(8,128)(2,1)} async-done(((bf16[16,68,2048]{2,1,0:T(8,128)(2,1)}), bf16[16,68,2048]{2,1,0:T(8,128)(2,1)}, u32[]{:S(2)}, u32[]{:S(2)}) %all-to-all-start) | async-done | bytes 4456480 | tf_op jit(solution)/shard_map/all_to_all | solution.py:131
  344.1 7.1 %reshape.111 = bf16[1088,2048]{1,0:T(8,128)(2,1)} reshape(bf16[16,68,2048]{2,1,0:T(8,128)(2,1)} %all-to-all-done) | data formatting | bytes 8912896 | tf_op jit(solution)/shard_map/reshape | solution.py:138
  351.2 8.0 %fusion.5 = f32[1088,1024]{1,0:T(8,128)S(1)} fusion(bf16[1088,2048]{1,0:T(8,128)(2,1)} %reshape.111, bf16[1,2048,1024]{2,1,0:T(8,128)(2,1)} %param.20), kind=kOutput, calls=%fused_computation.9 | convolution fusion | flops 4563402752 | bytes 13107200 | tf_op jit(solution)/shard_map/dot_general | solution.py:82
  359.2 4.3 convolution_convert_fusion.1
  363.6 3.3 multiply_convert_fusion.2
  366.9 6.2 %convolution_convert_fusion = bf16[2048,1024]{0,1:T(8,128)(2,1)S(1)} fusion(bf16[1088,2048]{1,0:T(8,128)(2,1)S(1)} %bitcast.89, bf16[1088,512]{1,0:T(8,128)(2,1)S(1)} %get-tuple-element.10, bf16[1088,512]{1,0:T(8,128)(2,1)S(1)} %get-tuple-element.9), kind=kOutput, calls=%fused_computation.21 | convolution fusion | flops 4569956352 | bytes 10878976 | tf_op jit(solution)/shard_map/dot_general | solution.py:98
  373.1 3.7 pad_maximum_fusion
  377.2 0.7 copy-done.4
  377.9 0.9 fusion.28
  378.8 92.4 %reduce-scatter.2.cloned.1.call-done = bf16[1024,1536]{0,1:T(8,128)(2,1)} async-done(((bf16[2048,1536]{0,1:T(8,128)(2,1)}), bf16[1024,1536]{0,1:T(8,128)(2,1)}) %reduce-scatter.2.cloned.1.call-update) | async-done | bytes 3145744 | tf_op jit(solution)/shard_map/reduce_scatter | solution.py:141
  471.2 2.6 convert_element_type.76
  473.8 1.6 slice_bitcast_fusion.1
  475.4 2.5 slice_bitcast_fusion
  477.9 5.5 %copy.38 = f32[1,1024,1024]{2,1,0:T(8,128)} copy(f32[1,1024,1024]{1,2,0:T(8,128)} %slice_bitcast_fusion) | data formatting | bytes 8388608
  483.4 2.9 copy.39
  (48 shorter events, 2.3 us)
Async XLA Ops:
  7.2 356.4 %copy-start = (bf16[1,2048,512]{2,1,0:T(8,128)(2,1)S(1)}, bf16[1,2048,512]{2,1,0:T(8,128)(2,1)}, u32[]{:S(2)}) copy-start(bf16[1,2048,512]{2,1,0:T(8,128)(2,1)} %param.21) | copy-start | bytes 6291460
  33.8 8.3 %copy-start.5 = (bf16[1,128,2048]{2,1,0:T(8,128)(2,1)S(1)}, bf16[1,128,2048]{2,1,0:T(8,128)(2,1)}, u32[]{:S(2)}) copy-start(bf16[1,128,2048]{2,1,0:T(8,128)(2,1)} %param.12) | copy-start | bytes 1572868
  33.8 216.7 %all-to-all-start.1 = ((bf16[16,68,2048]{2,1,0:T(8,128)(2,1)}), bf16[16,68,2048]{2,1,0:T(8,128)(2,1)}, u32[]{:S(2)}, u32[]{:S(2)}) async-start(bf16[16,68,2048]{2,1,0:T(8,128)(2,1)} %reshape.112), calls=%async_computation.1 | async-start | bytes 9437184 | tf_op jit(solution)/shard_map/all_to_all | solution.py:134
  41.3 178.6 %all-gather.2.cloned.1.call-start = ((), (), s32[]{:S(2)}) async-start(), calls=%async_computation.3 | async-start | bytes 2621440 | tf_op jit(solution)/shard_map/all_gather | solution.py:116
  42.4 125.4 %collective-permute-start = (bf16[1,128,2048]{1,2,0:T(8,128)(2,1)S(1)}, bf16[1,128,2048]{1,2,0:T(8,128)(2,1)}, u32[]{:S(2)}, u32[]{:S(2)}) collective-permute-start(bf16[1,128,2048]{1,2,0:T(8,128)(2,1)S(1)} %copy.23), channel_id=1, source_target_pairs={{0,4},{4,8},{8,12},{12,0},{1,5},{5,9},{9,13},{13,1},{2,6},{6,10},{... | collective-permute-start | bytes 1572872 | tf_op jit(solution)/shard_map/ppermute | solution.py:21
  44.3 162.3 %collective-permute-start.1 = (bf16[1,128,2048]{1,2,0:T(8,128)(2,1)S(1)}, bf16[1,128,2048]{1,2,0:T(8,128)(2,1)}, u32[]{:S(2)}, u32[]{:S(2)}) collective-permute-start(bf16[1,128,2048]{1,2,0:T(8,128)(2,1)S(1)} %copy.23), channel_id=1, source_target_pairs={{0,12},{4,0},{8,4},{12,8},{1,13},{5,1},{9,5},{13,9},{2,14},{6,2},{... | collective-permute-start | bytes 1572872 | tf_op jit(solution)/shard_map/ppermute | solution.py:24
  167.8 44.8 %collective-permute-start.2 = (bf16[1,128,2048]{1,2,0:T(8,128)(2,1)}, bf16[1,128,2048]{1,2,0:T(8,128)(2,1)}, u32[]{:S(2)}, u32[]{:S(2)}) collective-permute-start(bf16[1,128,2048]{1,2,0:T(8,128)(2,1)} %collective-permute-done), channel_id=1, source_target_pairs={{0,4},{4,8},{8,12},{12,0},{1,5},{5,9},{9,13},{13,1},{2,6},{6,10},{... | collective-permute-start | bytes 1572872 | tf_op jit(solution)/shard_map/ppermute | solution.py:21
  216.9 2.0 copy-start.2
  229.8 3.0 copy-start.6
  250.5 93.6 %all-to-all-start = ((bf16[16,68,2048]{2,1,0:T(8,128)(2,1)}), bf16[16,68,2048]{2,1,0:T(8,128)(2,1)}, u32[]{:S(2)}, u32[]{:S(2)}) async-start(bf16[16,68,2048]{2,1,0:T(8,128)(2,1)} %reshape.110), calls=%async_computation | async-start | bytes 9437184 | tf_op jit(solution)/shard_map/all_to_all | solution.py:131
  257.3 213.9 %reduce-scatter.2.cloned.1.call-start = ((), (), s32[]{:S(2)}) async-start(), calls=%async_computation.4 | async-start | bytes 9437184 | tf_op jit(solution)/shard_map/reduce_scatter | solution.py:141
  344.1 15.1 %slice-start = ((s8[4456448]{0:T(1024)(128)(4,1)}), s8[262144]{0:T(1024)(128)(4,1)S(1)}, s32[]{:S(2)}) async-start(s8[4456448]{0:T(1024)(128)(4,1)} %bitcast.86), calls=%async_computation.5 | async-start | bytes 524288
  351.2 8.0 %slice-start.1 = ((s8[4456448]{0:T(1024)(128)(4,1)}), s8[4194304]{0:T(1024)(128)(4,1)S(1)}, s32[]{:S(2)}) async-start(s8[4456448]{0:T(1024)(128)(4,1)} %bitcast.86), calls=%async_computation.6 | async-start | bytes 8388608
  359.2 7.7 %slice-start.2 = ((s8[4456448]{0:T(1024)(128)(4,1)}), s8[4194304]{0:T(1024)(128)(4,1)S(1)}, s32[]{:S(2)}) async-start(s8[4456448]{0:T(1024)(128)(4,1)} %bitcast.88), calls=%async_computation.7 | async-start | bytes 8388608
  363.6 3.3 slice-start.3
  366.9 6.3 %copy-start.3 = (bf16[2048,512]{0,1:T(8,128)(2,1)S(1)}, bf16[2048,512]{0,1:T(8,128)(2,1)}, u32[]{:S(2)}) copy-start(bf16[2048,512]{0,1:T(8,128)(2,1)} %convolution_convert_fusion.1) | copy-start | bytes 6291460
  376.9 1.0 copy-start.4
  477.9 8.4 %copy-start.1 = (bf16[1,2048,512]{2,1,0:T(8,128)(2,1)S(1)}, bf16[1,2048,512]{2,1,0:T(8,128)(2,1)}, u32[]{:S(2)}) copy-start(bf16[1,2048,512]{2,1,0:T(8,128)(2,1)} %param.21) | copy-start | bytes 6291460
Sparse Core Ops, SparseCore 0:
  43.8 104.0 all-gather.1
  377.0 94.1 reduce-scatter.1
